TPU v7x, 32 devices: a whole 2x2x4 slice. The times are simulated.
32 devices in a mesh: dp: 16 (over z, y, x), tensor: 2 (over core).
Axes of the slice: x: 2, y: 2, z: 4, core: 2. Of those that a mesh axis runs over, the one named last changes fastest.
Arguments:
- activations: bfloat16 [8192, 8192], P('dp', 'tensor'), may hold values from -6 to 6
- out_grads: bfloat16 [8192, 16384], P('dp', 'tensor'), may hold values from -0.0625 to 0.0625
- sketch: float32 [8192, 512], P('dp'), may hold values from -6 to 6
- first_moment: float32 [512, 16384], P('dp', 'tensor'), may hold values from -6 to 6
- second_moment: float32 [512, 16384], P('dp', 'tensor'), may hold values from 0.05 to 2
Outputs:
- update: float32 [8192, 16384], P('dp', 'tensor')
- first_new: float32 [512, 16384], P('dp', 'tensor')
- second_new: float32 [512, 16384], P('dp', 'tensor')
All inputs are finite; a program needn't handle non-finite values.
Results may differ from a plain program's by a relative error of at most 0.0041.
Values may be sent and summed in bfloat16 or wider, within the bound.
No kernel may reach another device: no remote copies, remote signals or barrier semaphores. Data moves between devices by JAX's collectives and lax.ppermute only.
A program may use at most 128 MiB of HBM per device.

v0:
```python
import math
import jax
import jax.numpy as jnp
from jax import lax
from jax.sharding import PartitionSpec as P

D = 8192
R = 512
BETA_ONE = 0.9
BETA_TWO = 0.999
CORRECT_ONE = 0.9999999993
CORRECT_TWO = 0.18135117
EPSILON = 1e-08


def local(activations, out_grads, sketch, first_moment, second_moment):
    highest = lax.Precision.HIGHEST
    features = lax.all_gather(activations, "tensor", axis=1, tiled=True)
    local_gram = jnp.dot(sketch.T, sketch, precision=highest, preferred_element_type=jnp.float32)
    sketch_gram = lax.psum(local_gram, "dp")
    cholesky_factor = jnp.linalg.cholesky(sketch_gram)
    own_rows = jax.scipy.linalg.solve_triangular(cholesky_factor, sketch.T, lower=True).T.astype(
        jnp.bfloat16
    )
    basis_full = lax.all_gather(own_rows, "dp", axis=0, tiled=True)
    projected = jnp.dot(features, basis_full, preferred_element_type=jnp.float32).astype(
        jnp.bfloat16
    )
    columns = projected
    grad_low = lax.psum_scatter(
        jnp.dot(columns.T, out_grads, preferred_element_type=jnp.float32),
        "dp",
        scatter_dimension=0,
        tiled=True,
    )
    first_new = BETA_ONE * first_moment + (1.0 - BETA_ONE) * grad_low
    second_new = BETA_TWO * second_moment + (1.0 - BETA_TWO) * grad_low * grad_low
    direction = (first_new / CORRECT_ONE / (jnp.sqrt(second_new / CORRECT_TWO) + EPSILON)).astype(
        jnp.bfloat16
    )
    update_scale = math.sqrt(D / R)
    columns = own_rows
    update = update_scale * jnp.dot(
        columns,
        lax.all_gather(direction, "dp", axis=0, tiled=True),
        preferred_element_type=jnp.float32,
    )
    return (update, first_new, second_new)


def solution(mesh):
    return jax.shard_map(
        local,
        mesh=mesh,
        in_specs=(
            P("dp", "tensor"),
            P("dp", "tensor"),
            P("dp", None),
            P("dp", "tensor"),
            P("dp", "tensor"),
        ),
        out_specs=(P("dp", "tensor"), P("dp", "tensor"), P("dp", "tensor")),
        check_vma=False,
    )
```

profile of v0, /device:TPU:0, one launch (start us, length us, event | category | flops | bytes accessed | tf_op | source)
XLA Modules:
  0.0 897.9 jit_solution(7498624918526684430)
XLA Ops:
  8.0 0.0 all-reduce.3.cloned.1.call-start
  8.0 4.5 fusion.38
  12.5 0.0 all-reduce.3.cloned.1.call-update
  12.5 0.0 copy-start
  12.5 0.0 all-gather.6.cloned.1.call-start
  12.6 0.5 all-gather.6.cloned.1.call-update
  13.1 0.0 all-gather.4.cloned.1.call-start
  13.2 115.9 %all-reduce.3.cloned.1.call-done = f32[512,512]{0,1:T(8,128)} async-done(((f32[512,512]{0,1:T(8,128)}), f32[512,512]{0,1:T(8,128)}) %all-reduce.3.cloned.1.call-update) | async-done | bytes 1048592 | tf_op jit(solution)/shard_map/psum | solution.py:20
  129.1 1.6 copy.9
  130.7 1.4 fusion.2
  132.2 11.7 %cholesky.104 = f32[128,128]{1,0:T(8,128)S(1)} custom-call(f32[128,128]{1,0:T(8,128)S(1)} %cholesky.266), custom_call_target="Cholesky" | custom-call | tf_op jit(solution)/shard_map/jit(cholesky)/cholesky | solution.py:21
  143.9 9.8 %custom-call.31 = f32[1,128,128]{1,2,0:T(8,128)S(1)} custom-call(f32[1,128,128]{2,1,0:T(8,128)S(1)} %get-tuple-element.33), custom_call_target="InvertDiagBlocksLowerTriangular" | custom-call | tf_op jit(solution)/shard_map/jit(cholesky)/cholesky | solution.py:21
  153.7 0.1 cholesky.224
  153.9 0.3 constant_dynamic-update-slice_fusion.3
  154.2 0.3 convolution_subtract_fusion.3
  154.5 11.7 %cholesky.217 = f32[128,128]{1,0:T(8,128)S(1)} custom-call(f32[128,128]{1,0:T(8,128)S(1)} %cholesky.270), custom_call_target="Cholesky" | custom-call | tf_op jit(solution)/shard_map/jit(cholesky)/cholesky | solution.py:21
  166.3 10.0 %custom-call.32 = f32[1,128,128]{1,2,0:T(8,128)S(1)} custom-call(f32[1,128,128]{2,1,0:T(8,128)S(1)} %get-tuple-element.30), custom_call_target="InvertDiagBlocksLowerTriangular" | custom-call | tf_op jit(solution)/shard_map/jit(cholesky)/cholesky | solution.py:21
  176.2 0.3 convolution_dynamic-update-slice_fusion
  176.5 0.4 convolution_subtract_fusion.4
  176.9 11.7 %cholesky.238 = f32[128,128]{1,0:T(8,128)S(1)} custom-call(f32[128,128]{1,0:T(8,128)S(1)} %cholesky.275), custom_call_target="Cholesky" | custom-call | tf_op jit(solution)/shard_map/jit(cholesky)/cholesky | solution.py:21
  188.7 9.8 %custom-call.33 = f32[1,128,128]{1,2,0:T(8,128)S(1)} custom-call(f32[1,128,128]{2,1,0:T(8,128)S(1)} %get-tuple-element.27), custom_call_target="InvertDiagBlocksLowerTriangular" | custom-call | tf_op jit(solution)/shard_map/jit(cholesky)/cholesky | solution.py:21
  198.5 0.2 convolution_dynamic-update-slice_fusion.1
  198.7 0.4 convolution_subtract_fusion.5
  199.1 11.7 %cholesky.255 = f32[128,128]{1,0:T(8,128)S(1)} custom-call(f32[128,128]{1,0:T(8,128)S(1)} %convolution_subtract_fusion.5), custom_call_target="Cholesky" | custom-call | tf_op jit(solution)/shard_map/jit(cholesky)/cholesky | solution.py:21
  210.8 0.7 compare_reduce_fusion.2
  212.7 0.6 compare_reduce_fusion.1
  214.1 0.6 compare_reduce_fusion
  215.3 0.3 select_select_fusion
  215.7 10.4 %while.1 = (s32[]{:T(128)}, f32[512,512]{1,0:T(8,128)S(1)}, s32[4,2]{0,1:T(2,128)S(1)}, f32[4,128,128]{2,1,0:T(8,128)}, s32[]{:T(128)}) while((s32[]{:T(128)}, f32[512,512]{1,0:T(8,128)S(1)}, s32[4,2]{0,1:T(2,128)S(1)}, f32[4,128,128]{2,1,0:T(8,128)}, s32[]{:T(128)}) %tuple.36), condition=%wide.while_cond, body=%wide.while_body.sunk | while | flops 2 | bytes 132205 | solution.py:22
  215.7 0.1 constant_dynamic-slice_fusion.2
  215.8 0.5 fusion.51
  216.3 2.0 bitcast_dynamic-update-slice_fusion.2
  218.3 0.1 constant_dynamic-slice_fusion.2
  218.4 0.5 fusion.51
  218.9 2.0 bitcast_dynamic-update-slice_fusion.2
  220.9 0.1 constant_dynamic-slice_fusion.2
  221.0 0.5 fusion.51
  221.5 2.0 bitcast_dynamic-update-slice_fusion.2
  223.5 0.1 constant_dynamic-slice_fusion.2
  223.6 0.5 fusion.51
  224.1 2.0 bitcast_dynamic-update-slice_fusion.2
  226.1 40.1 %custom-call.34 = f32[4,128,128]{1,2,0:T(8,128)S(1)} custom-call(f32[4,128,128]{2,1,0:T(8,128)} %get-tuple-element.10), custom_call_target="InvertDiagBlocksLowerTriangular" | custom-call | tf_op jit(solution)/shard_map/jit(_solve_triangular)/triangular_solve | solution.py:22
  266.2 0.0 copy-done
  266.2 0.4 fusion.37
  266.7 0.6 convolution_subtract_fusion.1
  267.3 0.4 fusion.36
  267.7 1.0 convolution_subtract_fusion
  268.7 0.4 fusion.35
  269.1 1.5 convolution_subtract_fusion.2
  270.6 0.4 convolution_convert_fusion.1
  271.0 0.8 fusion.21
  271.8 0.0 all-gather.4.cloned.1.call-update
  271.9 0.0 reduce-scatter.2.cloned.1.call-start
  271.9 0.0 all-gather.6.cloned.1.call-done
  272.0 120.0 %all-gather.4.cloned.1.call-done = bf16[8192,512]{0,1:T(8,128)(2,1)} async-done(((bf16[512,512]{0,1:T(8,128)(2,1)}), bf16[8192,512]{0,1:T(8,128)(2,1)}) %all-gather.4.cloned.1.call-update) | async-done | bytes 8388624 | tf_op jit(solution)/shard_map/all_gather | solution.py:25
  391.9 19.7 %fusion = f32[512,8192]{1,0:T(8,128)} fusion(bf16[512,8192]{1,0:T(8,128)(2,1)} %param.6, bf16[8192,512]{0,1:T(8,128)(2,1)} %all-gather.4.cloned.1.call-done, bf16[512,8192]{1,0:T(8,128)(2,1)} %all-gather.6.cloned.1.call-done), kind=kOutput, calls=%fused_computation.5 | convolution fusion | flops 8590196736 | bytes 41943040 | tf_op jit(solution)/shard_map/dot_general | solution.py:31
  411.6 0.0 reduce-scatter.2.cloned.1.call-update
  411.7 0.3 all-gather.8.cloned.1.call-start
  412.0 344.4 %reduce-scatter.2.cloned.1.call-done = f32[32,8192]{1,0:T(8,128)} async-done(((f32[512,8192]{1,0:T(8,128)}), f32[32,8192]{1,0:T(8,128)}) %reduce-scatter.2.cloned.1.call-update) | async-done | bytes 1048592 | tf_op jit(solution)/shard_map/reduce_scatter | solution.py:30
  756.4 0.0 copy-done.1
  756.4 3.0 divide_convert_fusion
  759.4 0.0 all-gather.8.cloned.1.call-update
  759.5 118.5 %all-gather.8.cloned.1.call-done = bf16[512,8192]{1,0:T(8,128)(2,1)} async-done(((bf16[32,8192]{1,0:T(8,128)(2,1)}), bf16[512,8192]{1,0:T(8,128)(2,1)}) %all-gather.8.cloned.1.call-update) | async-done | bytes 8388624 | tf_op jit(solution)/shard_map/all_gather | solution.py:45
  877.9 11.9 %convolution_multiply_fusion = f32[512,8192]{1,0:T(8,128)} fusion(bf16[512,8192]{1,0:T(8,128)(2,1)} %all-gather.8.cloned.1.call-done, bf16[128,512]{1,0:T(8,128)(2,1)S(1)} %convolution_convert_fusion.1, bf16[128,512]{1,0:T(8,128)(2,1)S(1)} %get-tuple-element.36, bf16[128,512]{1,0:T(8,128)(2,1)S(1)} %get-tuple-element.38, ...), kind=kOutput, calls=%fused_computation.2 | convolution fusion | flops 4301258752 | bytes 25690112 | tf_op jit(solution)/shard_map/dot_general | solution.py:43
  (13 shorter events, 0.2 us)
Async XLA Ops:
  8.0 121.1 %all-reduce.3.cloned.1.call-start = ((), (), s32[]{:S(2)}) async-start(), calls=%async_computation.1 | async-start | bytes 2097152 | tf_op jit(solution)/shard_map/psum | solution.py:20
  12.5 253.7 %copy-start = (f32[512,512]{1,0:T(8,128)S(1)}, f32[512,512]{1,0:T(8,128)}, u32[]{:S(2)}) copy-start(f32[512,512]{1,0:T(8,128)} %param.7) | copy-start | bytes 3145732
  12.5 259.4 %all-gather.6.cloned.1.call-start = ((), (), s32[]{:S(2)}) async-start(), calls=%async_computation.3 | async-start | bytes 12582912 | tf_op jit(solution)/shard_map/all_gather | solution.py:18
  13.1 378.8 %all-gather.4.cloned.1.call-start = ((), (), s32[]{:S(2)}) async-start(), calls=%async_computation.2 | async-start | bytes 8912896 | tf_op jit(solution)/shard_map/all_gather | solution.py:25
  271.9 484.5 %reduce-scatter.2.cloned.1.call-start = ((), (), s32[]{:S(2)}) async-start(), calls=%async_computation.4 | async-start | bytes 17825792 | tf_op jit(solution)/shard_map/reduce_scatter | solution.py:30
  411.6 344.8 %copy-start.1 = (f32[32,8192]{1,0:T(8,128)S(1)}, f32[32,8192]{1,0:T(8,128)}, u32[]{:S(2)}) copy-start(f32[32,8192]{1,0:T(8,128)} %param.9) | copy-start | bytes 3145732
  411.6 344.8 %copy-start.2 = (f32[32,8192]{1,0:T(8,128)S(1)}, f32[32,8192]{1,0:T(8,128)}, u32[]{:S(2)}) copy-start(f32[32,8192]{1,0:T(8,128)} %param.8) | copy-start | bytes 3145732
  411.7 466.3 %all-gather.8.cloned.1.call-start = ((), (), s32[]{:S(2)}) async-start(), calls=%async_computation.5 | async-start | bytes 8912896 | tf_op jit(solution)/shard_map/all_gather | solution.py:45
Sparse Core Ops, SparseCore 0:
  14.7 114.4 all-reduce.2
  411.8 344.5 reduce-scatter.1
Sparse Core Ops, SparseCore 1:
  14.6 22.4 all-gather.5
  272.0 119.9 all-gather.3
  759.5 118.4 all-gather.7
where the time goes:
time: 908 us; the launch traced here: 898 us
  waiting for transfers between devices  699 us (77%)
  other arithmetic  124 us (14%)
  matrix products  42.7 us (5%)
  between operations  18.9 us (2%)
  local copies, waits for them, and re-layouts  12.1 us (1%)
    reduce_scatter x1, waiting for transfers between devices, local(): lax.psum_scatter(jnp.dot(columns.T, out_grads, preferred_element_type=jnp...  344 us
    all_gather x1, waiting for transfers between devices, local(): basis_full = lax.all_gather(own_rows, 'dp', axis=0, tiled=True)  120 us
    all_gather x1, waiting for transfers between devices, local(): lax.all_gather(direction, 'dp', axis=0, tiled=True)  118 us
    psum x1, waiting for transfers between devices, local(): sketch_gram = lax.psum(local_gram, 'dp')  116 us
    another operation x14, other arithmetic, local(): cholesky_factor = jnp.linalg.cholesky(sketch_gram)  78.5 us
    another operation x3, other arithmetic, local(): jax.scipy.linalg.solve_triangular(cholesky_factor, sketch.T, lower=True)  40.5 us
    dot_general x1, matrix products, local(): jnp.dot(columns.T, out_grads, preferred_element_type=jnp.float32)  19.7 us
  transfers between devices with their start and end apart: 5, of which 4 were waited for; matrix products, arithmetic and copies ran while one was open for 16% of the time, Pallas kernels for 0%

commit v1 on v0

--- a/solution.py
+++ b/solution.py
@@ -17,7 +17,7 @@
     highest = lax.Precision.HIGHEST
     features = lax.all_gather(activations, "tensor", axis=1, tiled=True)
     local_gram = jnp.dot(sketch.T, sketch, precision=highest, preferred_element_type=jnp.float32)
-    sketch_gram = lax.psum(local_gram, "dp")
+    sketch_gram = jnp.sum(lax.all_gather(local_gram, "dp"), axis=0)
     cholesky_factor = jnp.linalg.cholesky(sketch_gram)
     own_rows = jax.scipy.linalg.solve_triangular(cholesky_factor, sketch.T, lower=True).T.astype(
         jnp.bfloat16

time: 908 us -> 994 us (1.095)
  waiting for transfers between devices: 699 us -> 777 us
    all_gather x0 -> x1, waiting for transfers between devices: none -> 194 us  [local(): sketch_gram = jnp.sum(lax.all_gather(local_gram, 'dp'), axis=0)]
    psum x1 -> x0, waiting for transfers between devices: 116 us -> none  [local(): sketch_gram = lax.psum(local_gram, 'dp')]
  transfers between devices with their start and end apart: 5 -> 5, of which waited for: 4 -> 4; matrix products, arithmetic and copies ran while one was open for 16% -> 15% of each run, Pallas kernels for 0% -> 0%
where the time goes in v1:
time: 994 us; the launch traced here: 984 us
  waiting for transfers between devices  777 us (78%)
  other arithmetic  131 us (13%)
  matrix products  46.3 us (5%)
  between operations  16.8 us (2%)
  local copies, waits for them, and re-layouts  11.9 us (1%)
    reduce_scatter x1, waiting for transfers between devices, local(): lax.psum_scatter(jnp.dot(columns.T, out_grads, preferred_element_type=jnp...  345 us
    all_gather x1, waiting for transfers between devices, local(): sketch_gram = jnp.sum(lax.all_gather(local_gram, 'dp'), axis=0)  194 us
    all_gather x1, waiting for transfers between devices, local(): basis_full = lax.all_gather(own_rows, 'dp', axis=0, tiled=True)  119 us
    all_gather x1, waiting for transfers between devices, local(): lax.all_gather(direction, 'dp', axis=0, tiled=True)  119 us
    another operation x14, other arithmetic, local(): cholesky_factor = jnp.linalg.cholesky(sketch_gram)  79 us
    another operation x3, other arithmetic, local(): jax.scipy.linalg.solve_triangular(cholesky_factor, sketch.T, lower=True)  40.3 us
  transfers between devices with their start and end apart: 5, of which 4 were waited for; matrix products, arithmetic and copies ran while one was open for 15% of the time, Pallas kernels for 0%

profile of v1, /device:TPU:0, one launch (start us, length us, event | category | flops | bytes accessed | tf_op | source)
XLA Modules:
  0.0 983.9 jit_solution(4174733418342251289)
XLA Ops:
  7.2 0.0 all-gather.12.cloned.1.call-start
  7.2 4.4 fusion.38
  11.7 0.0 all-gather.12.cloned.1.call-update
  11.7 0.0 all-gather.8.cloned.1.call-start
  11.7 0.7 all-gather.8.cloned.1.call-update
  12.4 0.0 all-gather.6.cloned.1.call-start
  12.5 193.7 %all-gather.12.cloned.1.call-done = f32[8192,512]{1,0:T(8,128)} async-done(((f32[512,512]{1,0:T(8,128)}), f32[8192,512]{1,0:T(8,128)}) %all-gather.12.cloned.1.call-update) | async-done | bytes 16777232 | tf_op jit(solution)/shard_map/all_gather | solution.py:20
  206.2 8.1 reduce_sum.9
  214.2 0.0 copy-start
  214.2 0.3 copy.9
  214.6 0.2 fusion.2
  214.8 1.0 copy-done.1
  215.8 11.7 %cholesky.104 = f32[128,128]{1,0:T(8,128)S(1)} custom-call(f32[128,128]{1,0:T(8,128)S(1)} %cholesky.266), custom_call_target="Cholesky" | custom-call | tf_op jit(solution)/shard_map/jit(cholesky)/cholesky | solution.py:21
  227.5 0.1 cholesky.224
  227.7 9.8 custom-call.31
  237.5 1.2 constant_dynamic-update-slice_fusion.3
  238.7 1.3 convolution_subtract_fusion.3
  240.0 12.2 %cholesky.217 = f32[128,128]{1,0:T(8,128)S(1)} custom-call(f32[128,128]{1,0:T(8,128)S(1)} %cholesky.270), custom_call_target="Cholesky" | custom-call | tf_op jit(solution)/shard_map/jit(cholesky)/cholesky | solution.py:21
  252.2 9.8 custom-call.32
  262.0 0.3 convolution_dynamic-update-slice_fusion
  262.3 1.3 convolution_subtract_fusion.4
  263.6 11.7 %cholesky.238 = f32[128,128]{1,0:T(8,128)S(1)} custom-call(f32[128,128]{1,0:T(8,128)S(1)} %cholesky.275), custom_call_target="Cholesky" | custom-call | tf_op jit(solution)/shard_map/jit(cholesky)/cholesky | solution.py:21
  275.3 9.8 custom-call.33
  285.2 0.2 convolution_dynamic-update-slice_fusion.1
  285.4 1.2 convolution_subtract_fusion.5
  286.6 11.9 %cholesky.255 = f32[128,128]{1,0:T(8,128)S(1)} custom-call(f32[128,128]{1,0:T(8,128)S(1)} %convolution_subtract_fusion.5), custom_call_target="Cholesky" | custom-call | tf_op jit(solution)/shard_map/jit(cholesky)/cholesky | solution.py:21
  298.5 0.7 compare_reduce_fusion.2
  300.4 0.6 compare_reduce_fusion.1
  301.8 0.6 compare_reduce_fusion
  303.1 0.1 select_select_fusion
  303.2 10.5 %while.1 = (s32[]{:T(128)}, f32[512,512]{1,0:T(8,128)S(1)}, s32[4,2]{0,1:T(2,128)S(1)}, f32[4,128,128]{2,1,0:T(8,128)}, s32[]{:T(128)}) while((s32[]{:T(128)}, f32[512,512]{1,0:T(8,128)S(1)}, s32[4,2]{0,1:T(2,128)S(1)}, f32[4,128,128]{2,1,0:T(8,128)}, s32[]{:T(128)}) %tuple.36), condition=%wide.while_cond, body=%wide.while_body.sunk | while | flops 2 | bytes 132205 | solution.py:22
  303.2 0.1 constant_dynamic-slice_fusion.2
  303.3 0.5 fusion.51
  303.8 2.0 bitcast_dynamic-update-slice_fusion.2
  305.8 0.1 constant_dynamic-slice_fusion.2
  305.9 0.5 fusion.51
  306.4 2.0 bitcast_dynamic-update-slice_fusion.2
  308.5 0.1 constant_dynamic-slice_fusion.2
  308.5 0.5 fusion.51
  309.1 2.0 bitcast_dynamic-update-slice_fusion.2
  311.1 0.1 constant_dynamic-slice_fusion.2
  311.1 0.5 fusion.51
  311.7 2.0 bitcast_dynamic-update-slice_fusion.2
  313.7 40.1 %custom-call.34 = f32[4,128,128]{1,2,0:T(8,128)S(1)} custom-call(f32[4,128,128]{2,1,0:T(8,128)} %get-tuple-element.10), custom_call_target="InvertDiagBlocksLowerTriangular" | custom-call | tf_op jit(solution)/shard_map/jit(_solve_triangular)/triangular_solve | solution.py:22
  353.8 0.4 fusion.37
  354.3 0.6 convolution_subtract_fusion.1
  354.9 0.4 fusion.36
  355.3 1.0 convolution_subtract_fusion
  356.3 0.4 fusion.35
  356.7 1.5 convolution_subtract_fusion.2
  358.2 0.4 convolution_convert_fusion.1
  358.6 0.8 fusion.21
  359.4 0.0 all-gather.6.cloned.1.call-update
  359.5 0.3 reduce-scatter.2.cloned.1.call-start
  359.7 0.0 all-gather.8.cloned.1.call-done
  359.8 119.3 %all-gather.6.cloned.1.call-done = bf16[8192,512]{0,1:T(8,128)(2,1)} async-done(((bf16[512,512]{0,1:T(8,128)(2,1)}), bf16[8192,512]{0,1:T(8,128)(2,1)}) %all-gather.6.cloned.1.call-update) | async-done | bytes 8388624 | tf_op jit(solution)/shard_map/all_gather | solution.py:25
  479.1 19.7 %fusion = f32[512,8192]{1,0:T(8,128)} fusion(bf16[512,8192]{1,0:T(8,128)(2,1)} %param.6, bf16[8192,512]{0,1:T(8,128)(2,1)} %all-gather.6.cloned.1.call-done, bf16[512,8192]{1,0:T(8,128)(2,1)} %all-gather.8.cloned.1.call-done), kind=kOutput, calls=%fused_computation.5 | convolution fusion | flops 8590196736 | bytes 41943040 | tf_op jit(solution)/shard_map/dot_general | solution.py:31
  498.8 0.0 reduce-scatter.2.cloned.1.call-update
  498.8 0.0 all-gather.10.cloned.1.call-start
  498.9 344.7 %reduce-scatter.2.cloned.1.call-done = f32[32,8192]{1,0:T(8,128)} async-done(((f32[512,8192]{1,0:T(8,128)}), f32[32,8192]{1,0:T(8,128)}) %reduce-scatter.2.cloned.1.call-update) | async-done | bytes 1048592 | tf_op jit(solution)/shard_map/reduce_scatter | solution.py:30
  843.5 3.0 divide_convert_fusion
  846.6 0.0 all-gather.10.cloned.1.call-update
  846.6 118.6 %all-gather.10.cloned.1.call-done = bf16[512,8192]{1,0:T(8,128)(2,1)} async-done(((bf16[32,8192]{1,0:T(8,128)(2,1)}), bf16[512,8192]{1,0:T(8,128)(2,1)}) %all-gather.10.cloned.1.call-update) | async-done | bytes 8388624 | tf_op jit(solution)/shard_map/all_gather | solution.py:45
  965.2 11.9 %convolution_multiply_fusion = f32[512,8192]{1,0:T(8,128)} fusion(bf16[512,8192]{1,0:T(8,128)(2,1)} %all-gather.10.cloned.1.call-done, bf16[128,512]{1,0:T(8,128)(2,1)S(1)} %convolution_convert_fusion.1, bf16[128,512]{1,0:T(8,128)(2,1)S(1)} %get-tuple-element.36, bf16[128,512]{1,0:T(8,128)(2,1)S(1)} %get-tuple-element.38, ...), kind=kOutput, calls=%fused_computation.2 | convolution fusion | flops 4301258752 | bytes 25690112 | tf_op jit(solution)/shard_map/dot_general | solution.py:43
  (16 shorter events, 0.2 us)
Async XLA Ops:
  7.2 199.0 %all-gather.12.cloned.1.call-start = ((), (), s32[]{:S(2)}) async-start(), calls=%async_computation.5 | async-start | bytes 17825792 | tf_op jit(solution)/shard_map/all_gather | solution.py:20
  11.7 348.1 %all-gather.8.cloned.1.call-start = ((), (), s32[]{:S(2)}) async-start(), calls=%async_computation.2 | async-start | bytes 12582912 | tf_op jit(solution)/shard_map/all_gather | solution.py:18
  12.4 466.6 %all-gather.6.cloned.1.call-start = ((), (), s32[]{:S(2)}) async-start(), calls=%async_computation.1 | async-start | bytes 8912896 | tf_op jit(solution)/shard_map/all_gather | solution.py:25
  214.2 139.6 %copy-start = (f32[512,512]{1,0:T(8,128)S(1)}, f32[512,512]{1,0:T(8,128)}, u32[]{:S(2)}) copy-start(f32[512,512]{1,0:T(8,128)} %param.7) | copy-start | bytes 3145732
  214.8 1.0 copy-start.1
  359.5 484.1 %reduce-scatter.2.cloned.1.call-start = ((), (), s32[]{:S(2)}) async-start(), calls=%async_computation.3 | async-start | bytes 17825792 | tf_op jit(solution)/shard_map/reduce_scatter | solution.py:30
  498.8 344.8 %copy-start.2 = (f32[32,8192]{1,0:T(8,128)S(1)}, f32[32,8192]{1,0:T(8,128)}, u32[]{:S(2)}) copy-start(f32[32,8192]{1,0:T(8,128)} %param.9) | copy-start | bytes 3145732
  498.8 344.8 %copy-start.3 = (f32[32,8192]{1,0:T(8,128)S(1)}, f32[32,8192]{1,0:T(8,128)}, u32[]{:S(2)}) copy-start(f32[32,8192]{1,0:T(8,128)} %param.8) | copy-start | bytes 3145732
  498.8 466.4 %all-gather.10.cloned.1.call-start = ((), (), s32[]{:S(2)}) async-start(), calls=%async_computation.4 | async-start | bytes 8912896 | tf_op jit(solution)/shard_map/all_gather | solution.py:45
Sparse Core Ops, SparseCore 0:
  11.8 194.3 all-gather.11
  207.7 18.0 all-gather.7
  359.6 119.4 all-gather.5
  498.9 344.5 reduce-scatter.1
  846.7 118.4 all-gather.9
